TPU v7x, 32 devices: a whole 2x2x4 slice. The times are simulated.
32 devices in a mesh: dir: 2 (over y), dp: 16 (over z, x, core).
Axes of the slice: x: 2, y: 2, z: 4, core: 2. Of those that a mesh axis runs over, the one named last changes fastest.
Arguments:
- tokens: bfloat16 [16, 1024, 768], P('dp', 'dir'), may hold values from -6 to 6
- norm_gain: float32 [768], replicated, may hold values from 0.5 to 1.5
- w_zx: bfloat16 [768, 3072], P('dp'), may hold values from -0.21875 to 0.21875
- w_bc: bfloat16 [768, 128], P('dp'), may hold values from -0.21875 to 0.21875
- w_dt: bfloat16 [768, 48], P('dp'), may hold values from -0.21875 to 0.21875
- conv_w: float32 [4, 1664], replicated, may hold values from -3 to 3
- conv_b: float32 [1664], replicated, may hold values from -1.75 to 1.75
- dt_bias: float32 [48], replicated, may hold values from -4.5 to -2
- a_log: float32 [48], replicated, may hold values from -2.5 to 1.5
- d_skip: float32 [24], replicated, may hold values from 0.5 to 1.5
- out_gain: float32 [1536], replicated, may hold values from 0.5 to 1.5
- w_out: bfloat16 [1536, 768], P('dp'), may hold values from -0.15625 to 0.15625
- doc_lengths: int32 [16, 4], P('dp'), may hold values from 1 to 512, 1024 in all within a row
- out_grad: bfloat16 [16, 1024, 768], P('dp', 'dir'), may hold values from -6 to 6
Outputs:
- block_out: bfloat16 [16, 1024, 768], P('dp', 'dir')
- grad_tokens: bfloat16 [16, 1024, 768], P('dp', 'dir')
- grad_norm_gain: float32 [768], replicated
- grad_w_zx: float32 [768, 3072], replicated
- grad_w_bc: float32 [768, 128], replicated
- grad_w_dt: float32 [768, 48], replicated
- grad_conv_w: float32 [4, 1664], replicated
- grad_conv_b: float32 [1664], replicated
- grad_dt_bias: float32 [48], replicated
- grad_a_log: float32 [48], replicated
- grad_d_skip: float32 [24], replicated
- grad_out_gain: float32 [1536], replicated
- grad_w_out: float32 [1536, 768], replicated
Inputs may be any that keep to these rules, and one draw needn't show every extreme that they name: `doc_lengths`: in each row the 4 lengths sum to 1024, and the longest is exactly 512.
All inputs are finite; a program needn't handle non-finite values.
Results may differ from a plain program's by a relative error of at most 0.014.
Values may be sent and summed in bfloat16 or wider, within the bound.
No kernel may reach another device: no remote copies, remote signals or barrier semaphores. Data moves between devices by JAX's collectives and lax.ppermute only.
A program may use at most 192 MiB of HBM per device.

v0:
```python
from functools import partial
import jax
import jax.numpy as jnp
from jax import lax
from jax.sharding import PartitionSpec as P

D = 768
HEADS = 24
HEADDIM = 64
STATE = 64
INNER = 1536
BLOCK = 128
CONV = 4
LEN = 1024
highest = lax.Precision.HIGHEST
epsilon = 1e-05


def shifted_2(block, axis, distance):
    devices = range(lax.axis_size(axis))
    route = [(i - distance, i) for i in devices if i - distance in devices]
    return lax.ppermute(block, axis, route)


def partner(shard, axis, stride):
    return lax.ppermute(shard, axis, [(i, i ^ 1 << stride) for i in range(lax.axis_size(axis))])


def segment_ids(lengths_row, length):
    doc_ends = jnp.cumsum(lengths_row)
    places = jnp.arange(length, dtype=jnp.int32)
    return jnp.sum((places[:, None] >= doc_ends[None, :]).astype(jnp.int32), axis=1)


def conv_silu(pre_conv, seg_row, conv_w, conv_b):
    tap_count = conv_w.shape[0]
    row_len = pre_conv.shape[0]
    padded = jnp.pad(pre_conv, ((tap_count - 1, 0), (0, 0)))
    seg_pad = jnp.concatenate([jnp.full((tap_count - 1,), -1, jnp.int32), seg_row], axis=0)
    summed = conv_b[None, :] + conv_w[tap_count - 1][None, :] * pre_conv
    for offset in range(1, tap_count):
        start = tap_count - 1 - offset
        shifted = padded[start : start + row_len]
        same_doc = (seg_pad[start : start + row_len] == seg_row)[:, None]
        summed = summed + jnp.where(
            same_doc, conv_w[tap_count - 1 - offset][None, :] * shifted, 0.0
        )
    return jax.nn.silu(summed)


def block_step(a_neg, carried, inputs):
    states, prev_seg = carried
    x_block, b_block, c_block, dt_block, seg_block = inputs
    block_len = x_block.shape[0]
    log_rates = dt_block * a_neg[None, :]
    cumul = jnp.cumsum(log_rates, axis=0)
    cum_heads = cumul.T
    places = jnp.arange(block_len, dtype=jnp.int32)
    keep_mask = (places[:, None] > places[None, :]) & (seg_block[:, None] == seg_block[None, :])
    scores = jnp.dot(c_block, b_block.T, precision=highest)
    weighted = jnp.where(
        keep_mask[None],
        jnp.exp(jnp.minimum(cum_heads[:, :, None] - cum_heads[:, None, :], 0.0)) * scores[None],
        0.0,
    )
    inputs_dt = x_block * dt_block[:, :, None]
    y_inner = jnp.einsum("hts,shp->thp", weighted, inputs_dt, precision=highest)
    carried_in = jnp.where((seg_block == prev_seg)[:, None], jnp.exp(cumul), 0.0)
    y_carry = jnp.einsum("tn,hpn->thp", c_block, states, precision=highest) * carried_in[:, :, None]
    last_seg = seg_block[block_len - 1]
    tail_weights = jnp.where(
        (seg_block == last_seg)[:, None], jnp.exp(cumul[block_len - 1][None, :] - cumul), 0.0
    )
    carry_keep = jnp.where(last_seg == prev_seg, jnp.exp(cumul[block_len - 1]), 0.0)
    new_states = states * carry_keep[:, None, None] + jnp.einsum(
        "shp,sn->hpn", inputs_dt * tail_weights[:, :, None], b_block, precision=highest
    )
    return ((new_states, last_seg), y_inner + y_carry)


def scan_dir(x_row, b_row, c_row, dt_row, a_neg, seg_row):
    length = x_row.shape[0]
    block_count = length // BLOCK
    head_count = dt_row.shape[1]
    head_width = x_row.shape[1] // head_count
    state_width = b_row.shape[1]
    sliced = (
        x_row.reshape(block_count, BLOCK, head_count, head_width),
        b_row.reshape(block_count, BLOCK, state_width),
        c_row.reshape(block_count, BLOCK, state_width),
        dt_row.reshape(block_count, BLOCK, head_count),
        seg_row.reshape(block_count, BLOCK),
    )
    initial = (
        jnp.zeros((head_count, head_width, state_width), x_row.dtype),
        jnp.array(-1, jnp.int32),
    )
    advance = jax.checkpoint(partial(block_step, a_neg))
    final_carry, results = lax.scan(advance, initial, sliced)
    return (results.reshape(length, head_count * head_width), final_carry[0])


def rms_scale(values, gain):
    return (
        values
        * lax.rsqrt(jnp.mean(values * values, axis=1, keepdims=True) + epsilon)
        * gain[None, :]
    )


def gate_norm(mixed_vals, gate_vals, gain):
    gated = mixed_vals * jax.nn.silu(gate_vals)
    return (
        gated * lax.rsqrt(jnp.mean(gated * gated, axis=1, keepdims=True) + epsilon) * gain[None, :]
    )


def body(
    tokens,
    norm_gain,
    w_zx,
    w_bc,
    w_dt,
    conv_w,
    conv_b,
    dt_bias,
    a_log,
    d_skip,
    out_gain,
    w_out,
    doc_lengths,
    out_grad,
):
    direction = lax.axis_index("dir")
    forward_side = direction == 0
    full_zx, full_bc, full_dt, full_out = (
        lax.all_gather(w_zx, "dp", axis=0, tiled=True),
        lax.all_gather(w_bc, "dp", axis=0, tiled=True),
        lax.all_gather(w_dt, "dp", axis=0, tiled=True),
        lax.all_gather(w_out, "dp", axis=0, tiled=True),
    )
    row_count = tokens.shape[0]
    half_len = tokens.shape[1]
    token_count = row_count * half_len
    x_flat = tokens.reshape(token_count, D).astype(jnp.float32)
    normed_f, rms_pull = jax.vjp(rms_scale, x_flat, norm_gain)
    normed = normed_f.astype(jnp.bfloat16)
    zx_proj = jnp.dot(normed, full_zx, preferred_element_type=jnp.float32)
    bc_proj = jnp.dot(normed, full_bc, preferred_element_type=jnp.float32)
    dt_proj = jnp.dot(normed, full_dt, preferred_element_type=jnp.float32).astype(jnp.bfloat16)
    gate_z = zx_proj[:, :INNER]
    pre_conv = jnp.concatenate([zx_proj[:, INNER:], bc_proj], axis=1).astype(jnp.bfloat16)
    seg_rows = jax.vmap(partial(segment_ids, length=LEN))(doc_lengths)
    pre_rows = pre_conv.reshape(row_count, half_len, INNER + 2 * STATE)
    dt_rows = dt_proj.reshape(row_count, half_len, 2 * HEADS)
    rim_len = CONV - 1
    rim_in = shifted_2(pre_rows[:, half_len - rim_len :, :], "dir", 1)
    pre_ext = jnp.concatenate([rim_in, pre_rows], axis=1).astype(jnp.float32)
    seg_padded = jnp.concatenate([jnp.full((row_count, rim_len), -1, jnp.int32), seg_rows], axis=1)
    seg_ext = lax.dynamic_slice_in_dim(seg_padded, direction * half_len, half_len + rim_len, 1)
    seam_fwd = seg_rows[:, half_len - 1]
    seam_rev = seg_rows[:, half_len]

    def local_mixer(pre_vals, dt_vals, conv_w_in, conv_b_in, bias_in, alog_in, skip_in):
        a_fwd = -jnp.exp(alog_in[:HEADS])
        a_rev = -jnp.exp(alog_in[HEADS:])
        skip_cols = jnp.repeat(skip_in, HEADDIM)

        def one_half(row_args):
            pre_row, dt_row, seg_row, fwd_seam, rev_seam = row_args
            conv_out = conv_silu(pre_row, seg_row, conv_w_in, conv_b_in)[rim_len:]
            seg_here = seg_row[rim_len:]
            dt_fwd = jax.nn.softplus(dt_row[:, :HEADS] + bias_in[None, :HEADS])
            dt_rev = jax.nn.softplus(dt_row[:, HEADS:] + bias_in[None, HEADS:])
            x_in = conv_out[:, :INNER]
            b_in = conv_out[:, INNER : INNER + STATE]
            c_in = conv_out[:, INNER + STATE :]
            y_fwd, state_fwd = scan_dir(x_in, b_in, c_in, dt_fwd, a_fwd, seg_here)
            y_flip, state_rev = scan_dir(
                jnp.flip(x_in, axis=0),
                jnp.flip(b_in, axis=0),
                jnp.flip(c_in, axis=0),
                jnp.flip(dt_rev, axis=0),
                a_rev,
                jnp.flip(seg_here, axis=0),
            )
            y_local = y_fwd + jnp.flip(y_flip, axis=0) + x_in * skip_cols[None, :]
            sending = jnp.where(forward_side, state_fwd, state_rev)
            cum_fwd = jnp.cumsum(dt_fwd * a_fwd[None, :], axis=0)
            cum_rev = jnp.flip(
                jnp.cumsum(jnp.flip(dt_rev * a_rev[None, :], axis=0), axis=0), axis=0
            )
            carry_rev = jnp.where((seg_here == rev_seam)[:, None], jnp.exp(cum_rev), 0.0)
            carry_fwd = jnp.where((seg_here == fwd_seam)[:, None], jnp.exp(cum_fwd), 0.0)
            carry_weight = jnp.where(forward_side, carry_rev, carry_fwd)
            return (y_local, sending, c_in, carry_weight)

        return lax.map(one_half, (pre_vals, dt_vals, seg_ext, seam_fwd, seam_rev))

    local_parts, local_pull = jax.vjp(
        local_mixer, pre_ext, dt_rows.astype(jnp.float32), conv_w, conv_b, dt_bias, a_log, d_skip
    )
    y_local, sending, c_kept, carry_kept = local_parts
    received = partner(sending.astype(jnp.bfloat16), "dir", 0).astype(sending.dtype)

    def seam_term(state_in, c_vals, weights):
        term = (
            jnp.einsum("rtn,rhpn->rthp", c_vals, state_in, precision=highest)
            * weights[:, :, :, None]
        )
        return term.reshape(row_count, half_len, INNER)

    correction, seam_pull = jax.vjp(seam_term, received, c_kept, carry_kept)
    mixed = y_local + correction
    mixed_flat = mixed.reshape(token_count, INNER)
    normed_out_f, gate_pull = jax.vjp(gate_norm, mixed_flat, gate_z, out_gain)
    normed_out = normed_out_f.astype(jnp.bfloat16)
    summed_out = x_flat + jnp.dot(normed_out, full_out, preferred_element_type=jnp.float32)
    block_out = summed_out.astype(jnp.bfloat16).reshape(row_count, half_len, D)
    grad_flat = out_grad.reshape(token_count, D)
    grad_w_out = jnp.einsum("tk,td->kd", normed_out, grad_flat, preferred_element_type=jnp.float32)
    grad_normed_out = jnp.einsum(
        "td,kd->tk", grad_flat, full_out, preferred_element_type=jnp.float32
    )
    grad_mixed, grad_gate, grad_out_gain = gate_pull(grad_normed_out)
    grad_mixed_low = grad_mixed.astype(jnp.bfloat16).reshape(row_count, half_len, INNER)
    grad_mixed_vals = grad_mixed_low.astype(jnp.float32)
    grad_received, grad_c_seam, grad_carry = seam_pull(grad_mixed_vals)
    grad_sending = partner(grad_received.astype(jnp.bfloat16), "dir", 0).astype(grad_received.dtype)
    grad_ext, grad_dt_half, grad_conv_w, grad_conv_b, grad_dt_bias, grad_a_log, grad_d_skip = (
        local_pull((grad_mixed_vals, grad_sending, grad_c_seam, grad_carry))
    )
    rim_back = shifted_2(grad_ext[:, :rim_len, :], "dir", -1)
    grad_pre_half = grad_ext[:, rim_len:, :] + jnp.pad(
        rim_back, ((0, 0), (half_len - rim_len, 0), (0, 0))
    )
    grad_pre_flat = grad_pre_half.reshape(token_count, INNER + 2 * STATE)
    grad_zx = jnp.concatenate([grad_gate, grad_pre_flat[:, :INNER]], axis=1).astype(jnp.bfloat16)
    grad_bc = grad_pre_flat[:, INNER:].astype(jnp.bfloat16)
    grad_dt_low = grad_dt_half.reshape(token_count, 2 * HEADS).astype(jnp.bfloat16)
    grad_w_zx = jnp.einsum("tk,tj->kj", normed, grad_zx, preferred_element_type=jnp.float32)
    grad_w_bc = jnp.einsum("tk,tj->kj", normed, grad_bc, preferred_element_type=jnp.float32)
    grad_w_dt = jnp.einsum("tk,tj->kj", normed, grad_dt_low, preferred_element_type=jnp.float32)
    grad_normed = (
        jnp.einsum("tj,kj->tk", grad_zx, full_zx, preferred_element_type=jnp.float32)
        + jnp.einsum("tj,kj->tk", grad_bc, full_bc, preferred_element_type=jnp.float32)
        + jnp.einsum("tj,kj->tk", grad_dt_low, full_dt, preferred_element_type=jnp.float32)
    )
    grad_x_norm, grad_norm_gain = rms_pull(grad_normed)
    grad_tokens = (
        (grad_flat.astype(jnp.float32) + grad_x_norm)
        .astype(jnp.bfloat16)
        .reshape(row_count, half_len, D)
    )
    (
        sum_norm_gain,
        sum_w_zx,
        sum_w_bc,
        sum_w_dt,
        sum_conv_w,
        sum_conv_b,
        sum_dt_bias,
        sum_a_log,
        sum_d_skip,
        sum_out_gain,
        sum_w_out,
    ) = lax.psum(
        (
            grad_norm_gain,
            grad_w_zx,
            grad_w_bc,
            grad_w_dt,
            grad_conv_w,
            grad_conv_b,
            grad_dt_bias,
            grad_a_log,
            grad_d_skip,
            grad_out_gain,
            grad_w_out,
        ),
        ("dir", "dp"),
    )
    return (
        block_out,
        grad_tokens,
        sum_norm_gain,
        sum_w_zx,
        sum_w_bc,
        sum_w_dt,
        sum_conv_w,
        sum_conv_b,
        sum_dt_bias,
        sum_a_log,
        sum_d_skip,
        sum_out_gain,
        sum_w_out,
    )


def solution(mesh):
    placed = (
        P("dp", "dir", None),
        P(),
        P("dp", None),
        P("dp", None),
        P("dp", None),
        P(),
        P(),
        P(),
        P(),
        P(),
        P(),
        P("dp", None),
        P("dp", None),
        P("dp", "dir", None),
    )
    return jax.shard_map(
        body,
        mesh=mesh,
        in_specs=placed,
        out_specs=(
            P("dp", "dir", None),
            P("dp", "dir", None),
            P(),
            P(),
            P(),
            P(),
            P(),
            P(),
            P(),
            P(),
            P(),
            P(),
            P(),
        ),
        check_vma=False,
    )
```

profile of v0, /device:TPU:0, one launch (start us, length us, event | category | flops | bytes accessed | tf_op | source)
XLA Modules:
  0.0 1082.4 jit_solution(1993637158967317221)
XLA Ops:
  10.2 24.4 %all_gather.14 = bf16[768,128]{1,0:T(8,128)(2,1)S(1)} all-gather(bf16[48,128]{1,0:T(8,128)(2,1)} %param.28), channel_id=1, replica_groups=mesh['dir'=2,'dp'=16] {'dp'}, dimensions={0}, use_global_device_ids=true | all-gather | bytes 208896 | tf_op jit(solution)/shard_map/all_gather | solution.py:138
  37.3 18.9 %all_gather.12 = bf16[768,48]{1,0:T(8,128)(2,1)S(1)} all-gather(bf16[48,48]{1,0:T(8,128)(2,1)} %param.29), channel_id=1, replica_groups=mesh['dir'=2,'dp'=16] {'dp'}, dimensions={0}, use_global_device_ids=true | all-gather | bytes 78336 | tf_op jit(solution)/shard_map/all_gather | solution.py:139
  67.4 4.6 fusion.288
  84.9 4.9 fusion.204
  93.8 24.7 %rev.107 = f32[512,1536]{1,0:T(8,128)} reverse(f32[512,1536]{1,0:T(8,128)} %slice.328), dimensions={0} | reverse | bytes 6291456 | tf_op jit(solution)/shard_map/jvp()/while/body/eval_jaxpr/jit(_flip)/rev | solution.py:180
  118.5 5.5 reshape.1386
  124.5 5.5 reshape.1387
  129.9 6.1 copy.490
  140.6 59.0 %while.230 = (s32[]{:T(128)}, f32[24,64,64]{2,1,0:T(8,128)S(1)}, s32[]{:T(128)}, f32[4,128,24,64]{1,3,2,0:T(8,128)}, f32[4,24,64,64]{3,2,1,0:T(8,128)}, /*index=...) while((s32[]{:T(128)}, f32[24,64,64]{2,1,0:T(8,128)S(1)}, ...), condition=%wide.region_8.10_spmd.clone, body=%wide.region_6.9_spmd.clone.sunk | while | flops 620061952 | bytes 7651091 | solution.py:99
  202.6 6.2 copy.484
  213.5 63.2 %while.229 = (s32[]{:T(128)}, f32[24,64,64]{2,1,0:T(8,128)S(1)}, s32[]{:T(128)}, f32[4,128,24,64]{1,3,2,0:T(8,128)}, f32[4,24,64,64]{3,2,1,0:T(8,128)}, /*index=...) while((s32[]{:T(128)}, f32[24,64,64]{2,1,0:T(8,128)S(1)}, ...), condition=%wide.region_5.7_spmd.clone, body=%wide.region_3.6_spmd.clone.sunk | while | flops 620061952 | bytes 7257875 | solution.py:99
  280.4 5.9 copy.544
  286.3 4.7 reshape.1381
  291.0 15.7 %rev.110 = f32[512,1536]{1,0:T(8,128)} reverse(f32[512,1536]{1,0:T(8,128)S(1)} %reshape.1381), dimensions={0} | reverse | bytes 6291456 | tf_op jit(solution)/shard_map/jvp()/while/body/eval_jaxpr/jit(_flip)/rev | solution.py:187
  306.7 5.9 copy.543
  312.6 6.3 reshape.1380
  318.9 5.2 broadcast_multiply_fusion.4
  327.7 7.1 multiply_reduce_fusion.16
  340.2 5.0 multiply_reduce_fusion.12
  345.7 5.7 multiply_reduce_fusion.13
  361.0 5.5 fusion.230
  371.7 5.0 reduce-window.64
  380.5 15.9 %reverse.3 = f32[512,1536]{1,0:T(8,128)} reverse(bf16[512,1536]{1,0:T(8,128)(2,1)S(1)} %get-tuple-element.2333), dimensions={0} | reverse | bytes 4718592 | tf_op jit(solution)/shard_map/reverse
  396.4 6.2 copy.519
  404.1 5.0 reduce-window.66
  413.3 6.1 copy.511
  424.7 144.4 %while.232 = (s32[]{:T(128)}, f32[24]{0:T(128)}, f32[24,64,64]{2,1,0:T(8,128)S(1)}, f32[4,128,24,64]{1,3,2,0:T(8,128)}, f32[4,128,64]{1,2,0:T(8,128)}, /*index=5...) while((s32[]{:T(128)}, f32[24]{0:T(128)}, ...), condition=%wide.region_40.42_spmd.clone, body=%wide.region_28.41_spmd.clone.sunk | while | flops 1408011520 | bytes 22274224 | solution.py:99
  438.4 4.8 multiply_reduce_fusion.28
  444.2 4.7 fusion.494
  474.4 4.8 multiply_reduce_fusion.28
  480.2 4.7 fusion.494
  510.3 4.8 multiply_reduce_fusion.28
  516.2 4.7 fusion.494
  546.3 4.8 multiply_reduce_fusion.28
  552.1 4.7 fusion.494
  574.8 142.2 %while.231 = (s32[]{:T(128)}, f32[24]{0:T(128)}, f32[24,64,64]{2,1,0:T(8,128)S(1)}, f32[4,128,24,64]{1,3,2,0:T(8,128)}, f32[4,128,64]{1,2,0:T(8,128)}, /*index=5...) while((s32[]{:T(128)}, f32[24]{0:T(128)}, ...), condition=%wide.region_27.29_spmd.clone, body=%wide.region_15.28_spmd.clone.sunk | while | flops 1408011520 | bytes 19111204 | solution.py:99
  588.5 4.5 multiply_reduce_fusion.25
  624.0 4.5 multiply_reduce_fusion.25
  725.9 5.8 copy.553
  731.7 6.3 reshape.1385
  742.0 6.2 reshape.1384
  748.2 24.7 %rev.115 = f32[512,1536]{1,0:T(8,128)} reverse(f32[512,1536]{1,0:T(8,128)} %reshape.1384), dimensions={0} | reverse | bytes 6291456 | tf_op jit(solution)/shard_map/transpose(jvp())/while/body/eval_jaxpr/jit(_flip)/rev | solution.py:180
  783.2 5.5 multiply_reduce_fusion.11
  800.1 5.6 fusion.210
  814.2 5.6 fusion.221
  819.8 42.1 %all-reduce.25 = (f32[768]{0:T(1024)}, f32[4,1664]{1,0:T(4,128)}, f32[1664]{0:T(1024)}, f32[48]{0:T(128)}, f32[48]{0:T(128)}, /*index=5*/f32[24]{0:T(128)}, f32[1536]{0:T(1024)}) all-reduce(f32[768]{0:T(1024)S(1)} %get-tuple-element.2195, f32[4,1664]{1,0:T(4,128)S(1)} %pad_add_fusion.3, ...), channel_id=1, replica_groups=mesh['dir'=2,'dp'=16] {'dir','dp'}, use_global_device_ids=true, to_apply=%region_48.50 | all-reduce | flops 10744 | bytes 85952 | tf_op jit(solution)/shard_map/psum | solution.py:267
  863.3 199.8 %all-reduce.29.cloned.1.call-done = (f32[768,3072]{1,0:T(8,128)}, f32[768,128]{1,0:T(8,128)}, f32[768,48]{0,1:T(8,128)}, f32[1536,768]{1,0:T(8,128)}) async-done(((f32[768,3072]{1,0:T(8,128)}, f32[768,128]{1,0:T(8,128)}, f32[768,48]{0,1:T(8,128)}, f32[1536,768]{1,0:T(8,128)}), (f32[768,3072]{1,0:T(8,128)}, f32[768,128]{1,0:T(8,128)}, f32[768,48]{0,1:T(8,128)}, ...) | async-done | bytes 14696464 | tf_op jit(solution)/shard_map/psum | solution.py:267
  1063.1 8.8 copy.749
  (959 shorter events, 479.6 us)
Async XLA Ops:
  7.2 50.6 %copy-start.20 = (bf16[1,512,768]{2,1,0:T(8,128)(2,1)S(1)}, bf16[1,512,768]{2,1,0:T(8,128)(2,1)}, u32[]{:S(2)}) copy-start(bf16[1,512,768]{2,1,0:T(8,128)(2,1)} %param.25) | copy-start | bytes 2359300
  7.2 50.6 %copy-start.65 = (f32[768]{0:T(1024)S(1)}, f32[768]{0:T(1024)}, u32[]{:S(2)}) copy-start(f32[768]{0:T(1024)} %param.26) | copy-start | bytes 9220
  7.2 51.2 %copy-start.120 = (f32[48]{0:T(128)S(1)}, f32[48]{0:T(128)}, u32[]{:S(2)}) copy-start(f32[48]{0:T(128)} %param.32) | copy-start | bytes 580
  7.2 51.2 %copy-start.112 = (f32[48]{0:T(128)S(1)}, f32[48]{0:T(128)}, u32[]{:S(2)}) copy-start(f32[48]{0:T(128)} %param.33) | copy-start | bytes 580
  7.2 60.2 %all-gather.3.cloned.1.call-start = ((), (), s32[]{:S(2)}) async-start(), calls=%async_computation | async-start | bytes 5013504 | tf_op jit(solution)/shard_map/all_gather | solution.py:137
  8.0 332.2 %all-gather.5.cloned.1.call-start = ((), (), s32[]{:S(2)}) async-start(), calls=%async_computation.1 | async-start | bytes 2506752 | tf_op jit(solution)/shard_map/all_gather | solution.py:140
  8.7 1054.4 %all-reduce.29.cloned.1.call-start = ((), (), s32[]{:S(2)}) async-start(), calls=%async_computation.2 | async-start | bytes 29392896 | tf_op jit(solution)/shard_map/psum | solution.py:267
  10.1 48.9 %copy-start.97 = (f32[512]{0:T(512)}, f32[512]{0:T(512)S(1)}, u32[]{:S(2)}) copy-start(f32[512]{0:T(512)S(1)} %fusion.222) | copy-start | bytes 6148
  10.1 61.9 %copy-start.70 = (f32[512]{0:T(512)}, f32[512]{0:T(512)S(1)}, u32[]{:S(2)}) copy-start(f32[512]{0:T(512)S(1)} %fusion.273) | copy-start | bytes 6148
  34.6 37.5 %copy-start.47 = (bf16[768,128]{1,0:T(8,128)(2,1)}, bf16[768,128]{1,0:T(8,128)(2,1)S(1)}, u32[]{:S(2)}) copy-start(bf16[768,128]{1,0:T(8,128)(2,1)S(1)} %all_gather.14) | copy-start | bytes 589828
  36.2 48.7 %copy-start.105 = (pred[515]{0:T(1024)(128)(4,1)}, pred[515]{0:T(1024)(128)(4,1)S(1)}, u32[]{:S(2)}) copy-start(pred[515]{0:T(1024)(128)(4,1)S(1)} %get-tuple-element.2392) | copy-start | bytes 1549
  36.2 48.7 %copy-start.107 = (pred[515]{0:T(1024)(128)(4,1)}, pred[515]{0:T(1024)(128)(4,1)S(1)}, u32[]{:S(2)}) copy-start(pred[515]{0:T(1024)(128)(4,1)S(1)} %get-tuple-element.2393) | copy-start | bytes 1549
  36.2 48.7 %copy-start.109 = (pred[515]{0:T(1024)(128)(4,1)}, pred[515]{0:T(1024)(128)(4,1)S(1)}, u32[]{:S(2)}) copy-start(pred[515]{0:T(1024)(128)(4,1)S(1)} %get-tuple-element.2394) | copy-start | bytes 1549
  37.2 47.7 %copy-start.80 = (f32[1664]{0:T(1024)}, f32[1664]{0:T(1024)S(1)}, u32[]{:S(2)}) copy-start(f32[1664]{0:T(1024)S(1)} %get-tuple-element.2197) | copy-start | bytes 19972
  37.2 47.7 %copy-start.82 = (f32[1664]{0:T(1024)}, f32[1664]{0:T(1024)S(1)}, u32[]{:S(2)}) copy-start(f32[1664]{0:T(1024)S(1)} %get-tuple-element.2198) | copy-start | bytes 19972
  37.2 47.7 %copy-start.84 = (f32[1664]{0:T(1024)}, f32[1664]{0:T(1024)S(1)}, u32[]{:S(2)}) copy-start(f32[1664]{0:T(1024)S(1)} %get-tuple-element.2199) | copy-start | bytes 19972
  37.2 47.7 %copy-start.86 = (f32[1664]{0:T(1024)}, f32[1664]{0:T(1024)S(1)}, u32[]{:S(2)}) copy-start(f32[1664]{0:T(1024)S(1)} %get-tuple-element.2200) | copy-start | bytes 19972
  56.2 15.8 %copy-start.49 = (bf16[768,48]{1,0:T(8,128)(2,1)}, bf16[768,48]{1,0:T(8,128)(2,1)S(1)}, u32[]{:S(2)}) copy-start(bf16[768,48]{1,0:T(8,128)(2,1)S(1)} %all_gather.12) | copy-start | bytes 221188
  57.8 25.9 %copy-start.42 = (bf16[512,128]{1,0:T(8,128)(2,1)}, bf16[512,128]{1,0:T(8,128)(2,1)S(1)}, u32[]{:S(2)}) copy-start(bf16[512,128]{1,0:T(8,128)(2,1)S(1)} %convolution_convert_fusion.1) | copy-start | bytes 393220
  59.0 13.1 %copy-start.118 = (f32[24]{0:T(128)}, f32[24]{0:T(128)S(1)}, u32[]{:S(2)}) copy-start(f32[24]{0:T(128)S(1)} %get-tuple-element.2410) | copy-start | bytes 292
  59.8 19.6 %copy-start.56 = (f32[512,24]{0,1:T(8,128)}, f32[512,24]{0,1:T(8,128)S(1)}, u32[]{:S(2)}) copy-start(f32[512,24]{0,1:T(8,128)S(1)} %get-tuple-element.2343) | copy-start | bytes 147460
  59.8 20.1 %copy-start.52 = (f32[512,24]{0,1:T(8,128)}, f32[512,24]{0,1:T(8,128)S(1)}, u32[]{:S(2)}) copy-start(f32[512,24]{0,1:T(8,128)S(1)} %get-tuple-element.2387) | copy-start | bytes 147460
  75.0 8.7 collective-permute-start
  81.6 246.0 %copy-start.78 = (f32[1536]{0:T(1024)}, f32[1536]{0:T(1024)S(1)}, u32[]{:S(2)}) copy-start(f32[1536]{0:T(1024)S(1)} %mul.1288) | copy-start | bytes 18436
  91.7 32.3 %copy-start.37 = (f32[512,64]{1,0:T(8,128)}, f32[512,64]{1,0:T(8,128)S(1)}, u32[]{:S(2)}) copy-start(f32[512,64]{1,0:T(8,128)S(1)} %get-tuple-element.2379) | copy-start | bytes 393220
  91.7 32.5 %copy-start.36 = (f32[512,64]{1,0:T(8,128)}, f32[512,64]{1,0:T(8,128)S(1)}, u32[]{:S(2)}) copy-start(f32[512,64]{1,0:T(8,128)S(1)} %get-tuple-element.2378) | copy-start | bytes 393220
  199.6 9.2 copy-start.28
  199.6 9.1 copy-start.33
  199.6 9.1 copy-start.34
  213.5 64.1 %copy-start.54 = (f32[512,24]{0,1:T(8,128)S(1)}, f32[512,24]{0,1:T(8,128)}, u32[]{:S(2)}) copy-start(f32[512,24]{0,1:T(8,128)} %rev.112) | copy-start | bytes 147460
  277.6 41.4 %collective-permute-start.1 = (bf16[1,24,64,64]{3,2,1,0:T(8,128)(2,1)}, bf16[1,24,64,64]{3,2,1,0:T(8,128)(2,1)}, u32[]{:S(2)}, u32[]{:S(2)}) collective-permute-start(bf16[1,24,64,64]{3,2,1,0:T(8,128)(2,1)} %fusion.246), channel_id=1, source_target_pairs={{0,16},{16,0},{1,17},{17,1},{2,18},{18,2},{3,19},{19,3},{4,20},{20... | collective-permute-start | bytes 589832 | tf_op jit(solution)/shard_map/ppermute | solution.py:26
  327.7 8.8 copy-start.30
  327.7 8.8 copy-start.76
  334.8 10.4 copy-start.94
  351.4 29.1 %copy-start.1 = (bf16[512,1536]{1,0:T(8,128)(2,1)}, bf16[512,1536]{1,0:T(8,128)(2,1)S(1)}, u32[]{:S(2)}) copy-start(bf16[512,1536]{1,0:T(8,128)(2,1)S(1)} %get-tuple-element.2333) | copy-start | bytes 4718596
  366.5 52.9 %collective-permute-start.2 = (bf16[1,24,64,64]{3,2,1,0:T(8,128)(2,1)}, bf16[1,24,64,64]{3,2,1,0:T(8,128)(2,1)}, u32[]{:S(2)}, u32[]{:S(2)}) collective-permute-start(bf16[1,24,64,64]{3,2,1,0:T(8,128)(2,1)} %fusion.230), channel_id=1, source_target_pairs={{0,16},{16,0},{1,17},{17,1},{2,18},{18,2},{3,19},{19,3},{4,20},{20... | collective-permute-start | bytes 589832 | tf_op jit(solution)/shard_map/ppermute | solution.py:26
  396.4 13.4 %copy-start.17 = (f32[512,1536]{1,0:T(8,128)S(1)}, f32[512,1536]{1,0:T(8,128)}, u32[]{:S(2)}) copy-start(f32[512,1536]{1,0:T(8,128)} %reverse.3) | copy-start | bytes 9437188
  748.2 24.7 %copy-start.45 = (f32[4,128,64]{2,1,0:T(8,128)S(1)}, f32[4,128,64]{2,1,0:T(8,128)}, u32[]{:S(2)}) copy-start(f32[4,128,64]{2,1,0:T(8,128)} %copy.522) | copy-start | bytes 393220
  748.2 24.7 %copy-start.46 = (f32[512,64]{1,0:T(8,128)S(1)}, f32[512,64]{1,0:T(8,128)}, u32[]{:S(2)}) copy-start(f32[512,64]{1,0:T(8,128)} %rev.114) | copy-start | bytes 393220
  748.2 24.7 %copy-start.2 = (bf16[512,1536]{1,0:T(8,128)(2,1)S(1)}, bf16[512,1536]{1,0:T(8,128)(2,1)}, u32[]{:S(2)}) copy-start(bf16[512,1536]{1,0:T(8,128)(2,1)} %copy-done.1) | copy-start | bytes 4718596
  748.2 24.7 %copy-start.79 = (f32[1536]{0:T(1024)S(1)}, f32[1536]{0:T(1024)}, u32[]{:S(2)}) copy-start(f32[1536]{0:T(1024)} %copy-done.78) | copy-start | bytes 18436
  791.5 5.7 collective-permute-start.3
  814.2 47.7 %copy-start.98 = (f32[512]{0:T(512)S(1)}, f32[512]{0:T(512)}, u32[]{:S(2)}) copy-start(f32[512]{0:T(512)} %copy-done.97) | copy-start | bytes 6148
  814.2 47.7 %copy-start.32 = (bf16[1,512,768]{2,1,0:T(8,128)(2,1)S(1)}, bf16[1,512,768]{2,1,0:T(8,128)(2,1)}, u32[]{:S(2)}) copy-start(bf16[1,512,768]{2,1,0:T(8,128)(2,1)} %param.38) | copy-start | bytes 2359300
  1063.1 10.2 slice-start
  1063.1 8.8 copy-start.60
  1063.1 9.5 copy-start.69
  1063.1 10.2 slice-start.1
  (134 other events, 619.7 us)
Sparse Core Ops, SparseCore 0:
  10.3 57.0 all-gather.2
  69.7 41.3 all-gather.4
  805.8 257.2 all-reduce.28
where the time goes:
time: 1100 us; the launch traced here: 1080 us
  local copies, waits for them, and re-layouts  336 us (31%)
  matrix products  265 us (24%)
  waiting for transfers between devices  207 us (19%)
  other arithmetic  142 us (13%)
  blocking collectives  85.5 us (8%)
  loops' own time  24 us (2%)
  between operations  15.6 us (1%)
    psum x1, waiting for transfers between devices, body(): lax.psum((grad_norm_gain, grad_w_zx, grad_w_bc, grad_w_dt, grad_conv_w, g...  200 us
    dot_general x24, matrix products, block_step(): y_inner = jnp.einsum('hts,shp->thp', weighted, inputs_dt, precision=highest)  108 us
    unnamed x228, local copies, waits for them, and re-layouts  52.9 us
    rev x2, local copies, waits for them, and re-layouts, one_half(): jnp.flip(x_in, axis=0)  49.4 us
    dot_general x32, matrix products, block_step(): jnp.einsum('tn,hpn->thp', c_block, states, precision=highest)  48.6 us
    dot_general x24, matrix products, block_step(): jnp.einsum('shp,sn->hpn', inputs_dt * tail_weights[:, :, None], b_block,...  48.2 us
    psum x1, blocking collectives, body(): lax.psum((grad_norm_gain, grad_w_zx, grad_w_bc, grad_w_dt, grad_conv_w, g...  42.1 us
    squeeze x48, local copies, waits for them, and re-layouts, scan_dir(): final_carry, results = lax.scan(advance, initial, sliced)  41.2 us
  transfers between devices with their start and end apart: 7, of which 3 were waited for; matrix products, arithmetic and copies ran while one was open for 30% of the time, Pallas kernels for 0%

commit v1 on v0

--- a/solution.py
+++ b/solution.py
@@ -14,6 +14,27 @@
 LEN = 1024
 highest = lax.Precision.HIGHEST
 epsilon = 1e-05
+
+
+def ring_gather(x, axis, dim):
+    devices, here, rows = (lax.axis_size(axis), lax.axis_index(axis), x.shape[dim])
+    forward = [(i, (i + 1) % devices) for i in range(devices)]
+    left = [(i, (i - 1) % devices) for i in range(devices)]
+    out = jnp.zeros((*x.shape[:dim], devices * rows, *x.shape[dim + 1 :]), x.dtype)
+    out = lax.dynamic_update_slice_in_dim(out, x, here * rows, axis=dim)
+    from_left = from_right = x
+    half = devices // 2
+    for hop in range(1, half + 1):
+        from_left = lax.ppermute(from_left, axis, forward)
+        out = lax.dynamic_update_slice_in_dim(
+            out, from_left, (here - hop) % devices * rows, axis=dim
+        )
+        if hop < devices - half:
+            from_right = lax.ppermute(from_right, axis, left)
+            out = lax.dynamic_update_slice_in_dim(
+                out, from_right, (here + hop) % devices * rows, axis=dim
+            )
+    return out
 
 
 def shifted_2(block, axis, distance):
@@ -135,7 +156,7 @@
     forward_side = direction == 0
     full_zx, full_bc, full_dt, full_out = (
         lax.all_gather(w_zx, "dp", axis=0, tiled=True),
-        lax.all_gather(w_bc, "dp", axis=0, tiled=True),
+        ring_gather(w_bc, "dp", 0),
         lax.all_gather(w_dt, "dp", axis=0, tiled=True),
         lax.all_gather(w_out, "dp", axis=0, tiled=True),
     )

time: 1100 us -> 1100 us (level)
  starting transfers between devices: 7 us -> 38.9 us
  blocking collectives: 85.5 us -> 60.5 us
  waiting for transfers between devices: 207 us -> 218 us
    ppermute x0 -> x15, starting transfers between devices: none -> 32.4 us  [the longest x7 31.4 us: ring_gather(): from_right = lax.ppermute(from_right, axis, left)]
    all_gather x1 -> x0, blocking collectives: 24.4 us -> none  [body(): lax.all_gather(w_bc, 'dp', axis=0, tiled=True)]
    ppermute x0 -> x15, waiting for transfers between devices: none -> 14.5 us  [the longest x8 14.4 us: ring_gather(): from_left = lax.ppermute(from_left, axis, forward)]
    unnamed x228 -> x232, local copies, waits for them, and re-layouts: 52.9 us -> 49.2 us
  transfers between devices with their start and end apart: 7 -> 22, of which waited for: 3 -> 9; matrix products, arithmetic and copies ran while one was open for 30% -> 29% of each run, Pallas kernels for 0% -> 0%
where the time goes in v1:
time: 1100 us; the launch traced here: 1090 us
  local copies, waits for them, and re-layouts  331 us (30%)
  matrix products  260 us (24%)
  waiting for transfers between devices  218 us (20%)
  other arithmetic  143 us (13%)
  blocking collectives  60.5 us (6%)
  starting transfers between devices  38.9 us (4%)
  loops' own time  24 us (2%)
  between operations  16.1 us (1%)
    psum x1, waiting for transfers between devices, body(): lax.psum((grad_norm_gain, grad_w_zx, grad_w_bc, grad_w_dt, grad_conv_w, g...  200 us
    dot_general x24, matrix products, block_step(): y_inner = jnp.einsum('hts,shp->thp', weighted, inputs_dt, precision=highest)  108 us
    rev x2, local copies, waits for them, and re-layouts, one_half(): jnp.flip(x_in, axis=0)  49.5 us
    unnamed x232, local copies, waits for them, and re-layouts  49.2 us
    dot_general x24, matrix products, block_step(): jnp.einsum('shp,sn->hpn', inputs_dt * tail_weights[:, :, None], b_block,...  48.2 us
    dot_general x32, matrix products, block_step(): jnp.einsum('tn,hpn->thp', c_block, states, precision=highest)  45.6 us
    squeeze x48, local copies, waits for them, and re-layouts, scan_dir(): final_carry, results = lax.scan(advance, initial, sliced)  41.2 us
    psum x1, blocking collectives, body(): lax.psum((grad_norm_gain, grad_w_zx, grad_w_bc, grad_w_dt, grad_conv_w, g...  39.8 us
  transfers between devices with their start and end apart: 22, of which 9 were waited for; matrix products, arithmetic and copies ran while one was open for 29% of the time, Pallas kernels for 0%

profile of v1, /device:TPU:0, one launch (start us, length us, event | category | flops | bytes accessed | tf_op | source)
XLA Modules:
  0.0 1090.5 jit_solution(8769417071026637926)
XLA Ops:
  8.5 5.0 collective-permute-start.1
  17.7 20.8 %all_gather.9 = bf16[768,48]{1,0:T(8,128)(2,1)S(1)} all-gather(bf16[48,48]{1,0:T(8,128)(2,1)} %param.29), channel_id=1, replica_groups=mesh['dir'=2,'dp'=16] {'dp'}, dimensions={0}, use_global_device_ids=true | all-gather | bytes 78336 | tf_op jit(solution)/shard_map/all_gather | solution.py:160
  59.3 4.6 collective-permute-start.7
  82.9 5.8 collective-permute-done.14
  89.2 4.6 fusion.287
  105.2 4.9 fusion.204
  113.0 24.8 %rev.107 = f32[512,1536]{1,0:T(8,128)} reverse(f32[512,1536]{1,0:T(8,128)} %slice.328), dimensions={0} | reverse | bytes 6291456 | tf_op jit(solution)/shard_map/jvp()/while/body/eval_jaxpr/jit(_flip)/rev | solution.py:201
  137.8 5.5 reshape.1386
  143.3 5.5 reshape.1387
  148.8 6.1 copy.490
  160.0 59.0 %while.230 = (s32[]{:T(128)}, f32[24,64,64]{2,1,0:T(8,128)S(1)}, s32[]{:T(128)}, f32[4,128,24,64]{1,3,2,0:T(8,128)}, f32[4,24,64,64]{3,2,1,0:T(8,128)}, /*index=...) while((s32[]{:T(128)}, f32[24,64,64]{2,1,0:T(8,128)S(1)}, ...), condition=%wide.region_8.10_spmd.clone, body=%wide.region_6.9_spmd.clone.sunk | while | flops 620061952 | bytes 7651091 | solution.py:120
  219.1 6.3 copy.484
  230.3 56.7 %while.229 = (s32[]{:T(128)}, f32[24,64,64]{2,1,0:T(8,128)S(1)}, s32[]{:T(128)}, f32[4,128,24,64]{1,3,2,0:T(8,128)}, f32[4,24,64,64]{3,2,1,0:T(8,128)}, /*index=...) while((s32[]{:T(128)}, f32[24,64,64]{2,1,0:T(8,128)S(1)}, ...), condition=%wide.region_5.7_spmd.clone, body=%wide.region_3.6_spmd.clone.sunk | while | flops 620061952 | bytes 7651091 | solution.py:120
  290.8 5.8 copy.544
  296.6 4.7 reshape.1381
  301.3 15.7 %rev.110 = f32[512,1536]{1,0:T(8,128)} reverse(f32[512,1536]{1,0:T(8,128)S(1)} %reshape.1381), dimensions={0} | reverse | bytes 6291456 | tf_op jit(solution)/shard_map/jvp()/while/body/eval_jaxpr/jit(_flip)/rev | solution.py:208
  317.0 5.8 copy.543
  322.9 6.3 reshape.1380
  329.2 5.2 broadcast_multiply_fusion.4
  338.0 7.1 multiply_reduce_fusion.16
  350.5 5.0 multiply_reduce_fusion.12
  356.0 5.7 multiply_reduce_fusion.13
  371.4 5.5 fusion.230
  382.0 5.0 reduce-window.64
  390.8 16.0 %reverse.3 = f32[512,1536]{1,0:T(8,128)} reverse(bf16[512,1536]{1,0:T(8,128)(2,1)S(1)} %get-tuple-element.2333), dimensions={0} | reverse | bytes 4718592 | tf_op jit(solution)/shard_map/reverse
  406.8 6.2 copy.519
  414.4 5.0 reduce-window.66
  423.6 6.1 copy.511
  435.0 143.7 %while.232 = (s32[]{:T(128)}, f32[24]{0:T(128)}, f32[24,64,64]{2,1,0:T(8,128)S(1)}, f32[4,128,24,64]{1,3,2,0:T(8,128)}, f32[4,128,64]{1,2,0:T(8,128)}, /*index=5...) while((s32[]{:T(128)}, f32[24]{0:T(128)}, ...), condition=%wide.region_40.42_spmd.clone, body=%wide.region_28.41_spmd.clone.sunk | while | flops 1408011520 | bytes 22274224 | solution.py:120
  448.7 4.8 multiply_reduce_fusion.28
  454.5 4.7 fusion.493
  484.5 4.8 multiply_reduce_fusion.28
  490.3 4.7 fusion.493
  520.3 4.8 multiply_reduce_fusion.28
  526.1 4.7 fusion.493
  556.1 4.8 multiply_reduce_fusion.28
  561.9 4.7 fusion.493
  584.5 142.4 %while.231 = (s32[]{:T(128)}, f32[24]{0:T(128)}, f32[24,64,64]{2,1,0:T(8,128)S(1)}, f32[4,128,24,64]{1,3,2,0:T(8,128)}, f32[4,128,64]{1,2,0:T(8,128)}, /*index=5...) while((s32[]{:T(128)}, f32[24]{0:T(128)}, ...), condition=%wide.region_27.29_spmd.clone, body=%wide.region_15.28_spmd.clone.sunk | while | flops 1408011520 | bytes 19111204 | solution.py:120
  735.8 5.8 copy.553
  741.6 6.3 reshape.1385
  751.9 6.2 reshape.1384
  758.1 24.7 %rev.115 = f32[512,1536]{1,0:T(8,128)} reverse(f32[512,1536]{1,0:T(8,128)} %reshape.1384), dimensions={0} | reverse | bytes 6291456 | tf_op jit(solution)/shard_map/transpose(jvp())/while/body/eval_jaxpr/jit(_flip)/rev | solution.py:201
  793.1 5.5 multiply_reduce_fusion.11
  810.0 5.6 fusion.210
  822.9 5.2 fusion.211
  830.0 39.8 %all-reduce.25 = (f32[768]{0:T(1024)}, f32[4,1664]{1,0:T(4,128)}, f32[1664]{0:T(1024)}, f32[48]{0:T(128)}, f32[48]{0:T(128)}, /*index=5*/f32[24]{0:T(128)}, f32[1536]{0:T(1024)}) all-reduce(f32[768]{0:T(1024)S(1)} %get-tuple-element.2195, f32[4,1664]{1,0:T(4,128)S(1)} %pad_add_fusion.3, ...), channel_id=1, replica_groups=mesh['dir'=2,'dp'=16] {'dir','dp'}, use_global_device_ids=true, to_apply=%region_48.50 | all-reduce | flops 10744 | bytes 85952 | tf_op jit(solution)/shard_map/psum | solution.py:288
  871.1 200.1 %all-reduce.29.cloned.1.call-done = (f32[768,3072]{1,0:T(8,128)}, f32[768,128]{1,0:T(8,128)}, f32[768,48]{0,1:T(8,128)}, f32[1536,768]{1,0:T(8,128)}) async-done(((f32[768,3072]{1,0:T(8,128)}, f32[768,128]{1,0:T(8,128)}, f32[768,48]{0,1:T(8,128)}, f32[1536,768]{1,0:T(8,128)}), (f32[768,3072]{1,0:T(8,128)}, f32[768,128]{1,0:T(8,128)}, f32[768,48]{0,1:T(8,128)}, ...) | async-done | bytes 14696464 | tf_op jit(solution)/shard_map/psum | solution.py:288
  1071.2 8.8 copy.826
  (1009 shorter events, 505.6 us)
Async XLA Ops:
  7.2 37.2 %copy-start.114 = (bf16[48,128]{1,0:T(8,128)(2,1)S(1)}, bf16[48,128]{1,0:T(8,128)(2,1)}, u32[]{:S(2)}) copy-start(bf16[48,128]{1,0:T(8,128)(2,1)} %param.28) | copy-start | bytes 36868
  7.2 81.5 %copy-start.17 = (bf16[1,512,768]{2,1,0:T(8,128)(2,1)S(1)}, bf16[1,512,768]{2,1,0:T(8,128)(2,1)}, u32[]{:S(2)}) copy-start(bf16[1,512,768]{2,1,0:T(8,128)(2,1)} %param.25) | copy-start | bytes 2359300
  7.2 81.5 %copy-start.68 = (f32[768]{0:T(1024)S(1)}, f32[768]{0:T(1024)}, u32[]{:S(2)}) copy-start(f32[768]{0:T(1024)} %param.26) | copy-start | bytes 9220
  7.2 82.0 %all-gather.3.cloned.1.call-start = ((), (), s32[]{:S(2)}) async-start(), calls=%async_computation | async-start | bytes 5013504 | tf_op jit(solution)/shard_map/all_gather | solution.py:158
  7.9 342.5 %all-gather.5.cloned.1.call-start = ((), (), s32[]{:S(2)}) async-start(), calls=%async_computation.1 | async-start | bytes 2506752 | tf_op jit(solution)/shard_map/all_gather | solution.py:161
  8.0 39.2 %collective-permute-start = (bf16[48,128]{1,0:T(8,128)(2,1)}, bf16[48,128]{1,0:T(8,128)(2,1)S(1)}, u32[]{:S(2)}, u32[]{:S(2)}) collective-permute-start(bf16[48,128]{1,0:T(8,128)(2,1)} %param.28), channel_id=1, source_target_pairs={{0,1},{1,2},{2,3},{3,4},{4,5},{5,6},{6,7},{7,8},{8,9},{9,10},{10,1... | collective-permute-start | bytes 36872 | tf_op jit(solution)/shard_map/ppermute | solution.py:28
  8.5 39.1 %collective-permute-start.1 = (bf16[48,128]{1,0:T(8,128)(2,1)}, bf16[48,128]{1,0:T(8,128)(2,1)S(1)}, u32[]{:S(2)}, u32[]{:S(2)}) collective-permute-start(bf16[48,128]{1,0:T(8,128)(2,1)} %param.28), channel_id=1, source_target_pairs={{0,15},{1,0},{2,1},{3,2},{4,3},{5,4},{6,5},{7,6},{8,7},{9,8},{10,9... | collective-permute-start | bytes 36872 | tf_op jit(solution)/shard_map/ppermute | solution.py:33
  13.6 1057.6 %all-reduce.29.cloned.1.call-start = ((), (), s32[]{:S(2)}) async-start(), calls=%async_computation.2 | async-start | bytes 29392896 | tf_op jit(solution)/shard_map/psum | solution.py:288
  15.0 78.8 %copy-start.72 = (f32[512]{0:T(512)}, f32[512]{0:T(512)S(1)}, u32[]{:S(2)}) copy-start(f32[512]{0:T(512)S(1)} %fusion.272) | copy-start | bytes 6148
  16.7 88.5 %copy-start.108 = (pred[515]{0:T(1024)(128)(4,1)}, pred[515]{0:T(1024)(128)(4,1)S(1)}, u32[]{:S(2)}) copy-start(pred[515]{0:T(1024)(128)(4,1)S(1)} %get-tuple-element.2392) | copy-start | bytes 1549
  16.7 88.5 %copy-start.110 = (pred[515]{0:T(1024)(128)(4,1)}, pred[515]{0:T(1024)(128)(4,1)S(1)}, u32[]{:S(2)}) copy-start(pred[515]{0:T(1024)(128)(4,1)S(1)} %get-tuple-element.2393) | copy-start | bytes 1549
  16.7 88.5 %copy-start.112 = (pred[515]{0:T(1024)(128)(4,1)}, pred[515]{0:T(1024)(128)(4,1)S(1)}, u32[]{:S(2)}) copy-start(pred[515]{0:T(1024)(128)(4,1)S(1)} %get-tuple-element.2394) | copy-start | bytes 1549
  17.7 87.5 %copy-start.83 = (f32[1664]{0:T(1024)}, f32[1664]{0:T(1024)S(1)}, u32[]{:S(2)}) copy-start(f32[1664]{0:T(1024)S(1)} %get-tuple-element.2197) | copy-start | bytes 19972
  17.7 87.5 %copy-start.85 = (f32[1664]{0:T(1024)}, f32[1664]{0:T(1024)S(1)}, u32[]{:S(2)}) copy-start(f32[1664]{0:T(1024)S(1)} %get-tuple-element.2198) | copy-start | bytes 19972
  17.7 87.5 %copy-start.87 = (f32[1664]{0:T(1024)}, f32[1664]{0:T(1024)S(1)}, u32[]{:S(2)}) copy-start(f32[1664]{0:T(1024)S(1)} %get-tuple-element.2199) | copy-start | bytes 19972
  17.7 87.5 %copy-start.89 = (f32[1664]{0:T(1024)}, f32[1664]{0:T(1024)S(1)}, u32[]{:S(2)}) copy-start(f32[1664]{0:T(1024)S(1)} %get-tuple-element.2200) | copy-start | bytes 19972
  42.5 58.2 %copy-start.59 = (f32[512,24]{0,1:T(8,128)}, f32[512,24]{0,1:T(8,128)S(1)}, u32[]{:S(2)}) copy-start(f32[512,24]{0,1:T(8,128)S(1)} %get-tuple-element.2343) | copy-start | bytes 147460
  42.5 58.7 %copy-start.55 = (f32[512,24]{0,1:T(8,128)}, f32[512,24]{0,1:T(8,128)S(1)}, u32[]{:S(2)}) copy-start(f32[512,24]{0,1:T(8,128)S(1)} %get-tuple-element.2387) | copy-start | bytes 147460
  47.2 6.1 collective-permute-start.2
  47.6 5.8 collective-permute-start.3
  53.4 5.9 collective-permute-start.4
  53.4 5.9 collective-permute-start.5
  59.3 6.0 collective-permute-start.6
  59.3 6.0 collective-permute-start.7
  65.4 5.8 collective-permute-start.8
  65.4 5.8 collective-permute-start.9
  71.2 5.8 collective-permute-start.10
  71.2 5.8 collective-permute-start.11
  77.0 5.8 collective-permute-start.12
  77.0 5.8 collective-permute-start.13
  82.8 5.9 collective-permute-start.14
  89.1 14.9 %copy-start.45 = (bf16[512,128]{1,0:T(8,128)(2,1)}, bf16[512,128]{1,0:T(8,128)(2,1)S(1)}, u32[]{:S(2)}) copy-start(bf16[512,128]{1,0:T(8,128)(2,1)S(1)} %convolution_convert_fusion.1) | copy-start | bytes 393220
  96.8 7.2 collective-permute-start.15
  101.7 186.2 %copy-start.57 = (f32[512,24]{0,1:T(8,128)}, f32[512,24]{0,1:T(8,128)S(1)}, u32[]{:S(2)}) copy-start(f32[512,24]{0,1:T(8,128)S(1)} %rev.112) | copy-start | bytes 147460
  101.8 236.1 %copy-start.81 = (f32[1536]{0:T(1024)}, f32[1536]{0:T(1024)S(1)}, u32[]{:S(2)}) copy-start(f32[1536]{0:T(1024)S(1)} %mul.1352) | copy-start | bytes 18436
  113.0 41.9 %copy-start.39 = (f32[512,64]{1,0:T(8,128)}, f32[512,64]{1,0:T(8,128)S(1)}, u32[]{:S(2)}) copy-start(f32[512,64]{1,0:T(8,128)S(1)} %get-tuple-element.2379) | copy-start | bytes 393220
  113.0 42.1 %copy-start.37 = (f32[512,64]{1,0:T(8,128)}, f32[512,64]{1,0:T(8,128)S(1)}, u32[]{:S(2)}) copy-start(f32[512,64]{1,0:T(8,128)S(1)} %get-tuple-element.2378) | copy-start | bytes 393220
  287.9 41.3 %collective-permute-start.16 = (bf16[1,24,64,64]{3,2,1,0:T(8,128)(2,1)}, bf16[1,24,64,64]{3,2,1,0:T(8,128)(2,1)}, u32[]{:S(2)}, u32[]{:S(2)}) collective-permute-start(bf16[1,24,64,64]{3,2,1,0:T(8,128)(2,1)} %fusion.246), channel_id=1, source_target_pairs={{0,16},{16,0},{1,17},{17,1},{2,18},{18,2},{3,19},{19,3},{4,20},{20... | collective-permute-start | bytes 589832 | tf_op jit(solution)/shard_map/ppermute | solution.py:47
  361.7 29.1 %copy-start.1 = (bf16[512,1536]{1,0:T(8,128)(2,1)}, bf16[512,1536]{1,0:T(8,128)(2,1)S(1)}, u32[]{:S(2)}) copy-start(bf16[512,1536]{1,0:T(8,128)(2,1)S(1)} %get-tuple-element.2333) | copy-start | bytes 4718596
  376.8 52.9 %collective-permute-start.17 = (bf16[1,24,64,64]{3,2,1,0:T(8,128)(2,1)}, bf16[1,24,64,64]{3,2,1,0:T(8,128)(2,1)}, u32[]{:S(2)}, u32[]{:S(2)}) collective-permute-start(bf16[1,24,64,64]{3,2,1,0:T(8,128)(2,1)} %fusion.230), channel_id=1, source_target_pairs={{0,16},{16,0},{1,17},{17,1},{2,18},{18,2},{3,19},{19,3},{4,20},{20... | collective-permute-start | bytes 589832 | tf_op jit(solution)/shard_map/ppermute | solution.py:47
  406.8 13.4 %copy-start.20 = (f32[512,1536]{1,0:T(8,128)S(1)}, f32[512,1536]{1,0:T(8,128)}, u32[]{:S(2)}) copy-start(f32[512,1536]{1,0:T(8,128)} %reverse.3) | copy-start | bytes 9437188
  758.1 24.7 %copy-start.48 = (f32[4,128,64]{2,1,0:T(8,128)S(1)}, f32[4,128,64]{2,1,0:T(8,128)}, u32[]{:S(2)}) copy-start(f32[4,128,64]{2,1,0:T(8,128)} %copy.522) | copy-start | bytes 393220
  758.1 24.7 %copy-start.49 = (f32[512,64]{1,0:T(8,128)S(1)}, f32[512,64]{1,0:T(8,128)}, u32[]{:S(2)}) copy-start(f32[512,64]{1,0:T(8,128)} %rev.114) | copy-start | bytes 393220
  758.1 24.7 %copy-start.2 = (bf16[512,1536]{1,0:T(8,128)(2,1)S(1)}, bf16[512,1536]{1,0:T(8,128)(2,1)}, u32[]{:S(2)}) copy-start(bf16[512,1536]{1,0:T(8,128)(2,1)} %copy-done.1) | copy-start | bytes 4718596
  758.1 24.7 %copy-start.82 = (f32[1536]{0:T(1024)S(1)}, f32[1536]{0:T(1024)}, u32[]{:S(2)}) copy-start(f32[1536]{0:T(1024)} %copy-done.81) | copy-start | bytes 18436
  801.4 5.7 collective-permute-start.18
  828.1 41.6 %copy-start.101 = (f32[512]{0:T(512)S(1)}, f32[512]{0:T(512)}, u32[]{:S(2)}) copy-start(f32[512]{0:T(512)} %copy-done.100) | copy-start | bytes 6148
  828.1 41.6 %copy-start.32 = (bf16[1,512,768]{2,1,0:T(8,128)(2,1)S(1)}, bf16[1,512,768]{2,1,0:T(8,128)(2,1)}, u32[]{:S(2)}) copy-start(bf16[1,512,768]{2,1,0:T(8,128)(2,1)} %param.38) | copy-start | bytes 2359300
  (151 other events, 733.2 us)
Sparse Core Ops, SparseCore 0:
  10.3 57.2 all-gather.2
  69.9 40.8 all-gather.4
  815.7 255.4 all-reduce.28
